TPU v7x, 128 devices: a whole 4x4x4 slice. The times are simulated.
128 devices in a mesh: req: 32 (over x, y, core), mlp: 4 (over z).
Axes of the slice: x: 4, y: 4, z: 4, core: 2. Of those that a mesh axis runs over, the one named last changes fastest.
Arguments:
- new_qkv: bfloat16 [1024, 3, 3072], P('req', None, 'mlp'), may hold values from -8 to 8
- prompt_cache: bfloat16 [32, 4096, 2, 3072], P('req', None, None, 'mlp'), may hold values from -6 to 6
- tail_cache: bfloat16 [512, 256, 2, 3072], P('req', None, None, 'mlp'), may hold values from -6 to 6
- residual: bfloat16 [1024, 3072], P('req', 'mlp'), may hold values from -6 to 6
- w_out: bfloat16 [3072, 3072], P('mlp'), may hold values from -0.109375 to 0.109375
- mlp_gain: float32 [3072], replicated, may hold values from 0.5 to 1.5
- w_gate: bfloat16 [3072, 8192], P(None, ('req', 'mlp')), may hold values from -0.109375 to 0.109375
- w_up: bfloat16 [3072, 8192], P(None, ('req', 'mlp')), may hold values from -0.109375 to 0.109375
- w_down: bfloat16 [8192, 3072], P(('req', 'mlp')), may hold values from -0.25 to 0.25
- final_gain: float32 [3072], replicated, may hold values from 0.5 to 1.5
- score_weight: float32 [3072], replicated, may hold values from -0.109375 to 0.109375
- slot_part: int32 [32], replicated, may hold values from 0 to 31, each once
- prompt_len: int32 [16], replicated, may hold values from 1 to 8192, 65536 in all
- tail_len: int32 [512], replicated, may hold values from 1 to 256, 65536 in all
Outputs:
- hidden_out: bfloat16 [1024, 3072], P('req', 'mlp')
- score: float32 [1024], P('req')
Inputs may be any that keep to these rules, and one draw needn't show every extreme that they name: Each value once; slot s holds half slot_part[s] % 2 of prompt slot_part[s] // 2. `prompt_len`: the largest is exactly 8192. `tail_len`: the largest is exactly 256.
All inputs are finite; a program needn't handle non-finite values.
Results may differ from a plain program's by a relative error of at most 0.015.
Values may be sent and summed in bfloat16 or wider, within the bound.
A program may use at most 192 MiB of HBM per device.

v0:
```python
import math
import jax
import jax.numpy as jnp
from jax import lax
from jax.sharding import PartitionSpec as P

HD = 96
norm_eps = 1e-05
masked_value = -1e30


def rotary(values, position):
    half_dim = HD // 2
    freqs = 10000.0 ** (-(jnp.arange(half_dim, dtype=jnp.float32) * 2.0) / HD)
    angles = position.astype(jnp.float32)[..., None] * freqs
    cosine = jnp.cos(angles)[..., None, :]
    sine = jnp.sin(angles)[..., None, :]
    first = values[..., :half_dim]
    second = values[..., half_dim:]
    return jnp.concatenate(
        [first * cosine - second * sine, second * cosine + first * sine], axis=-1
    )


def per_device(
    new_qkv,
    prompt_cache,
    tail_cache,
    residual,
    w_out,
    mlp_gain,
    w_gate,
    w_up,
    w_down,
    final_gain,
    score_weight,
    slot_part,
    prompt_len,
    tail_len,
):
    req_count = lax.axis_size("req")
    req_index = lax.axis_index("req")
    mlp_index = lax.axis_index("mlp")
    rows_here = new_qkv.shape[0]
    width_here = new_qkv.shape[2]
    heads_here = width_here // HD
    conts_here = rows_here // 2
    width = w_out.shape[1]
    score_scale = 1.0 / math.sqrt(HD)
    own_prompt = req_index // 2
    tail_here = lax.dynamic_slice_in_dim(tail_len, req_index * conts_here, conts_here)
    plen_here = lax.dynamic_index_in_dim(prompt_len, own_prompt, 0, keepdims=False)
    position = plen_here + tail_here[:, None] + jnp.arange(2, dtype=jnp.int32)[None, :]
    block = new_qkv.reshape(conts_here, 2, 3, heads_here, HD)
    query = rotary(block[:, :, 0].astype(jnp.float32), position).astype(jnp.bfloat16)
    key_new = rotary(block[:, :, 1].astype(jnp.float32), position).astype(jnp.bfloat16)
    value_new = block[:, :, 2]
    gathered = lax.all_gather(query.reshape(rows_here, width_here), "req", axis=0, tiled=True)
    slot_ids = jnp.arange(req_count, dtype=jnp.int32)
    slot_of = jnp.sum(
        jnp.where(slot_part[None, :] == slot_ids[:, None], slot_ids[None, :], 0), axis=1
    )
    held_part = lax.dynamic_index_in_dim(slot_part, req_index, 0, keepdims=False)
    owned_prompt = held_part // 2
    held_half = held_part % 2
    span = prompt_cache.shape[1]
    owned_rows = 2 * rows_here
    q_owned = lax.dynamic_slice_in_dim(gathered, owned_prompt * owned_rows, owned_rows, 0).reshape(
        owned_rows, heads_here, HD
    )
    owned_len = lax.dynamic_index_in_dim(prompt_len, owned_prompt, 0, keepdims=False)
    valid_count = jnp.clip(owned_len - held_half * span, 0, span)
    block_len = min(512, span)
    block_count = (valid_count + block_len - 1) // block_len
    cache_keys = prompt_cache[0, :, 0].reshape(span, heads_here, HD)
    cache_values = prompt_cache[0, :, 1].reshape(span, heads_here, HD)

    def score_block(number, buffer):
        key_block = lax.dynamic_slice_in_dim(cache_keys, number * block_len, block_len, 0)
        block_scores = (
            jnp.einsum("rhd,khd->hrk", q_owned, key_block, preferred_element_type=jnp.float32)
            * score_scale
        )
        places = number * block_len + jnp.arange(block_len, dtype=jnp.int32)
        block_scores = jnp.where(places[None, None, :] < valid_count, block_scores, masked_value)
        return lax.dynamic_update_slice_in_dim(buffer, block_scores, number * block_len, 2)

    empty_scores = jnp.full((heads_here, owned_rows, span), masked_value, jnp.float32)
    prefix_scores = lax.fori_loop(0, block_count, score_block, empty_scores)
    prefix_max = jnp.max(prefix_scores, axis=2)

    def value_block(number, carry):
        numer, totals = carry
        score_part = lax.dynamic_slice_in_dim(prefix_scores, number * block_len, block_len, 2)
        weights = jnp.exp(score_part - prefix_max[:, :, None])
        value_part = lax.dynamic_slice_in_dim(cache_values, number * block_len, block_len, 0)
        numer = numer + jnp.einsum(
            "hrk,khd->rhd",
            weights.astype(jnp.bfloat16),
            value_part,
            preferred_element_type=jnp.float32,
        )
        return (numer, totals + jnp.sum(weights, axis=2))

    start_carry = (
        jnp.zeros((owned_rows, heads_here, HD), jnp.float32),
        jnp.zeros((heads_here, owned_rows), jnp.float32),
    )
    owner_numer, owner_total = lax.fori_loop(0, block_count, value_block, start_carry)
    packed = jnp.concatenate(
        [
            owner_numer.reshape(owned_rows, width_here),
            jnp.transpose(owner_total),
            jnp.transpose(prefix_max),
        ],
        axis=1,
    )
    packed_all = lax.all_gather(packed[None], "req", axis=0, tiled=True)
    row_offset = req_index % 2 * rows_here
    slot_first = lax.dynamic_index_in_dim(slot_of, 2 * own_prompt, 0, keepdims=False)
    slot_second = lax.dynamic_index_in_dim(slot_of, 2 * own_prompt + 1, 0, keepdims=False)

    def part_of(slot):
        piece = lax.dynamic_slice_in_dim(
            lax.dynamic_index_in_dim(packed_all, slot, 0, keepdims=False), row_offset, rows_here, 0
        )
        numer = piece[:, :width_here].reshape(rows_here, heads_here, HD)
        total = piece[:, width_here : width_here + heads_here]
        top = piece[:, width_here + heads_here :]
        return (numer, total, top)

    numer_first, total_first, max_first = part_of(slot_first)
    numer_second, total_second, max_second = part_of(slot_second)
    tail_cap = tail_cache.shape[1]
    tail_keys = tail_cache[:, :, 0].reshape(conts_here, tail_cap, heads_here, HD)
    tail_values = tail_cache[:, :, 1].reshape(conts_here, tail_cap, heads_here, HD)
    s_tail = (
        jnp.einsum("cthd,cjhd->chtj", query, tail_keys, preferred_element_type=jnp.float32)
        * score_scale
    )
    s_tail = jnp.where(
        jnp.arange(tail_cap)[None, None, None, :] < tail_here[:, None, None, None],
        s_tail,
        masked_value,
    )
    s_new = (
        jnp.einsum("cthd,cuhd->chtu", query, key_new, preferred_element_type=jnp.float32)
        * score_scale
    )
    causal = jnp.arange(2)[None, :] <= jnp.arange(2)[:, None]
    s_new = jnp.where(causal[None, None, :, :], s_new, masked_value)
    tail_max = jnp.maximum(jnp.max(s_tail, -1), jnp.max(s_new, -1))
    w_tail = jnp.exp(s_tail - tail_max[..., None])
    w_new = jnp.exp(s_new - tail_max[..., None])
    numer_tail = jnp.einsum(
        "chtj,cjhd->cthd",
        w_tail.astype(jnp.bfloat16),
        tail_values,
        preferred_element_type=jnp.float32,
    )
    numer_tail = numer_tail + jnp.einsum(
        "chtu,cuhd->cthd", w_new.astype(jnp.bfloat16), value_new, preferred_element_type=jnp.float32
    )
    numer_tail = numer_tail.reshape(rows_here, heads_here, HD)
    total_tail = jnp.transpose(jnp.sum(w_tail, -1) + jnp.sum(w_new, -1), (0, 2, 1)).reshape(
        rows_here, heads_here
    )
    max_tail = jnp.transpose(tail_max, (0, 2, 1)).reshape(rows_here, heads_here)
    row_max = jnp.maximum(jnp.maximum(max_first, max_second), max_tail)
    scale_first = jnp.exp(max_first - row_max)
    scale_second = jnp.exp(max_second - row_max)
    scale_tail = jnp.exp(max_tail - row_max)
    row_total = total_first * scale_first + total_second * scale_second + total_tail * scale_tail
    row_numer = (
        numer_first * scale_first[..., None]
        + numer_second * scale_second[..., None]
        + numer_tail * scale_tail[..., None]
    )
    attn = (row_numer / row_total[:, :, None]).astype(jnp.bfloat16).reshape(rows_here, width_here)
    residual_full = lax.all_gather(residual, "mlp", axis=1, tiled=True)
    projected = lax.psum(jnp.dot(attn, w_out, preferred_element_type=jnp.float32), "mlp")
    state = residual_full.astype(jnp.float32) + projected
    mean_square = jnp.mean(state * state, axis=1, keepdims=True)
    normed = (state * lax.rsqrt(mean_square + norm_eps) * mlp_gain).astype(jnp.bfloat16)
    mlp_count = lax.axis_size("mlp")
    share = rows_here // mlp_count
    normed_share = lax.dynamic_slice_in_dim(normed, mlp_index * share, share, 0)
    piece = lax.all_gather(normed_share, "req", axis=0, tiled=True)
    gate_w = lax.all_gather(w_gate, "mlp", axis=1, tiled=True)
    up_w = lax.all_gather(w_up, "mlp", axis=1, tiled=True)
    down_w = lax.all_gather(w_down, "mlp", axis=0, tiled=True)
    gate = jnp.dot(piece, gate_w, preferred_element_type=jnp.float32)
    upper = jnp.dot(piece, up_w, preferred_element_type=jnp.float32)
    hidden_all = (jax.nn.silu(gate) * upper).astype(jnp.bfloat16)
    row_sums = lax.psum_scatter(
        jnp.dot(hidden_all, down_w, preferred_element_type=jnp.float32),
        "req",
        scatter_dimension=0,
        tiled=True,
    )
    state_share = lax.dynamic_slice_in_dim(state, mlp_index * share, share, 0)
    final_share = state_share + row_sums
    final_square = jnp.mean(final_share * final_share, axis=1)
    final_dot = jnp.sum(final_share * final_gain * score_weight, axis=1)
    score_share = final_dot * lax.rsqrt(final_square + norm_eps)
    scores = lax.all_gather(score_share, "mlp", axis=0, tiled=True)
    out_rows = lax.all_to_all(
        final_share.astype(jnp.bfloat16), "mlp", split_axis=1, concat_axis=0, tiled=True
    )
    return (out_rows, scores)


def solution(mesh):
    in_specs = (
        P("req", None, "mlp"),
        P("req", None, None, "mlp"),
        P("req", None, None, "mlp"),
        P("req", "mlp"),
        P("mlp", None),
        P(),
        P(None, ("req", "mlp")),
        P(None, ("req", "mlp")),
        P(("req", "mlp"), None),
        P(),
        P(),
        P(),
        P(),
        P(),
    )
    out_specs = (P("req", "mlp"), P("req"))
    return jax.shard_map(
        per_device, mesh=mesh, in_specs=in_specs, out_specs=out_specs, check_vma=False
    )
```

profile of v0, /device:TPU:0, one launch (start us, length us, event | category | flops | bytes accessed | tf_op | source)
XLA Modules:
  0.0 547.5 jit_solution(2006875817612300921)
XLA Ops:
  17.5 24.7 %fusion.44 = (bf16[1,4096,1,768]{3,2,1,0:T(2,128)(2,1)}, bf16[1,4096,1,768]{3,2,1,0:T(2,128)(2,1)}) fusion(bf16[1,4096,2,768]{3,2,1,0:T(2,128)(2,1)} %param.19), kind=kLoop, calls=%fused_computation.90 | loop fusion | bytes 25165824 | tf_op jit(solution)/shard_map/slice | solution.py:76
  42.2 27.2 %copy.87 = bf16[1,4096,1,768]{1,3,2,0:T(8,128)(2,1)} copy(bf16[1,4096,1,768]{3,2,1,0:T(2,128)(2,1)} %get-tuple-element.154) | data formatting | bytes 12582912 | tf_op jit(solution)/shard_map/slice | solution.py:75
  69.4 27.0 %copy.86 = bf16[1,4096,1,768]{1,3,2,0:T(8,128)(2,1)} copy(bf16[1,4096,1,768]{3,2,1,0:T(2,128)(2,1)} %get-tuple-element.153) | data formatting | bytes 12582912 | tf_op jit(solution)/shard_map/slice | solution.py:76
  97.5 4.2 broadcast_in_dim.60
  101.8 9.7 %while.22 = (s32[]{:T(128)}, f32[8,64,4096]{2,1,0:T(8,128)}, s32[]{:T(128)}, s32[]{:T(128)}, bf16[4096,8,96]{0,2,1:T(8,128)(2,1)}, /*index=5*/bf16[64,8,96]{2,0,...) while((s32[]{:T(128)}, f32[8,64,4096]{2,1,0:T(8,128)}, s32[]{:T(128)}, s32[]{:T(128)}, ...), condition=%wide.region_1.2_spmd, body=%wide.region_0.1_spmd.sunk | while | flops 50856964 | bytes 1935515 | solution.py:89
  111.4 3.8 reduce_max.27
  115.3 14.2 %while.23 = (s32[]{:T(128)}, f32[64,8,96]{2,0,1:T(8,128)S(1)}, f32[8,64]{1,0:T(8,128)S(1)}, s32[]{:T(128)}, bf16[4096,8,96]{0,2,1:T(8,128)(2,1)}, /*index=5*/f32...) while((s32[]{:T(128)}, f32[64,8,96]{2,0,1:T(8,128)S(1)}, ...), condition=%wide.region_5.6_spmd, body=%wide.region_3.5_spmd.sunk | while | flops 51429380 | bytes 3290271 | solution.py:109
  134.1 25.7 %fusion.43 = (bf16[16,256,1,768]{3,2,1,0:T(2,128)(2,1)}, bf16[16,256,1,768]{3,2,1,0:T(2,128)(2,1)}) fusion(bf16[16,256,2,768]{3,2,1,0:T(2,128)(2,1)} %param.20), kind=kLoop, calls=%fused_computation.89 | loop fusion | bytes 25165824 | tf_op jit(solution)/shard_map/slice | solution.py:136
  159.9 29.2 %copy.94 = bf16[16,256,1,768]{1,3,0,2:T(8,128)(2,1)} copy(bf16[16,256,1,768]{3,2,1,0:T(2,128)(2,1)} %get-tuple-element.152) | data formatting | bytes 12582912 | tf_op jit(solution)/shard_map/slice | solution.py:135
  190.1 3.8 fusion.48
  194.3 29.2 %copy.99 = bf16[16,256,1,768]{1,3,0,2:T(8,128)(2,1)} copy(bf16[16,256,1,768]{3,2,1,0:T(2,128)(2,1)} %get-tuple-element.151) | data formatting | bytes 12582912 | tf_op jit(solution)/shard_map/slice | solution.py:136
  223.8 4.6 fusion.15
  232.6 4.0 fusion.34
  237.3 13.5 %all_gather.24 = bf16[32,3072]{1,0:T(8,128)(2,1)S(1)} all-gather(bf16[32,768]{1,0:T(8,128)(2,1)S(1)} %copy-done), channel_id=1, replica_groups=mesh['req'=32,'mlp'=4] {'mlp'}, dimensions={1}, use_global_device_ids=true | all-gather | bytes 245760 | tf_op jit(solution)/shard_map/all_gather | solution.py:180
  250.7 54.6 %all-reduce.3.cloned.1.call-done = f32[32,3072]{1,0:T(8,128)} async-done(((f32[32,3072]{1,0:T(8,128)}), f32[32,3072]{1,0:T(8,128)}) %all-reduce.3.cloned.1.call-update) | async-done | bytes 393232 | tf_op jit(solution)/shard_map/psum | solution.py:181
  308.7 25.4 %all-gather.12.cloned.1.call-done = bf16[3072,256]{0,1:T(8,128)(2,1)} async-done(((bf16[3072,64]{0,1:T(8,128)(2,1)}), bf16[3072,256]{0,1:T(8,128)(2,1)}) %all-gather.12.cloned.1.call-update) | async-done | bytes 1572880 | tf_op jit(solution)/shard_map/all_gather | solution.py:189
  334.0 46.0 %all-gather.10.cloned.1.call-done = bf16[256,3072]{1,0:T(8,128)(2,1)} async-done(((bf16[8,3072]{1,0:T(8,128)(2,1)}), bf16[256,3072]{1,0:T(8,128)(2,1)}) %all-gather.10.cloned.1.call-update) | async-done | bytes 1572880 | tf_op jit(solution)/shard_map/all_gather | solution.py:188
  380.0 2.5 fusion.49
  382.5 25.2 %all-gather.14.cloned.1.call-done = bf16[3072,256]{0,1:T(8,128)(2,1)} async-done(((bf16[3072,64]{0,1:T(8,128)(2,1)}), bf16[3072,256]{0,1:T(8,128)(2,1)}) %all-gather.14.cloned.1.call-update) | async-done | bytes 1572880 | tf_op jit(solution)/shard_map/all_gather | solution.py:190
  407.8 28.5 %all-gather.16.cloned.1.call-done = bf16[256,3072]{1,0:T(8,128)(2,1)} async-done(((bf16[64,3072]{1,0:T(8,128)(2,1)}), bf16[256,3072]{1,0:T(8,128)(2,1)}) %all-gather.16.cloned.1.call-update) | async-done | bytes 1572880 | tf_op jit(solution)/shard_map/all_gather | solution.py:191
  436.2 5.8 %fusion.14 = f32[256,3072]{1,0:T(8,128)} fusion(bf16[256,3072]{1,0:T(8,128)(2,1)} %all-gather.16.cloned.1.call-done, bf16[256,3072]{1,0:T(8,128)(2,1)} %all-gather.10.cloned.1.call-done, bf16[3072,256]{0,1:T(8,128)(2,1)} %all-gather.14.cloned.1.call-done, f32[256,256]{1,0:T(8,128)S(1)} %fusion.49), kind=kOutput, calls=%fused_computation.19 | convolution fusion | flops 805699584 | bytes 8126464 | tf_op jit(solution)/shard_map/dot_general | solution.py:196
  443.4 79.1 %reduce-scatter.2.cloned.1.call-done = f32[8,3072]{1,0:T(8,128)} async-done(((f32[256,3072]{1,0:T(8,128)}), f32[8,3072]{1,0:T(8,128)}) %reduce-scatter.2.cloned.1.call-update) | async-done | bytes 98320 | tf_op jit(solution)/shard_map/reduce_scatter | solution.py:195
  524.1 4.4 all-to-all-start
  528.6 11.4 %all-reduce = f32[32]{0:T(128)} all-reduce(f32[32]{0:T(128)S(1)} %multiply_dynamic-update-slice_fusion), channel_id=1, replica_groups=mesh['req'=32,'mlp'=4] {'mlp'}, use_global_device_ids=true, to_apply=%add | all-reduce | flops 32 | bytes 256
  (114 shorter events, 45.2 us)
Async XLA Ops:
  7.2 89.3 %all-gather.8.cloned.1.call-start = ((), (), s32[]{:S(2)}) async-start(), calls=%async_computation.2 | async-start | bytes 1622016 | tf_op jit(solution)/shard_map/all_gather | solution.py:58
  16.8 213.9 %all-gather.18.cloned.1.call-start = ((), (), s32[]{:S(2)}) async-start(), calls=%async_computation.9 | async-start | bytes 7569408 | tf_op jit(solution)/shard_map/all_gather | solution.py:118
  115.3 15.5 %copy-start.4 = (s32[32]{0:T(128)S(1)}, s32[32]{0:T(128)}, u32[]{:S(2)}) copy-start(s32[32]{0:T(128)} %param.29) | copy-start | bytes 388
  130.8 174.5 %all-reduce.3.cloned.1.call-start = ((), (), s32[]{:S(2)}) async-start(), calls=%async_computation.3 | async-start | bytes 786432 | tf_op jit(solution)/shard_map/psum | solution.py:181
  228.4 8.9 %copy-start = (bf16[32,768]{1,0:T(8,128)(2,1)S(1)}, bf16[32,768]{1,0:T(8,128)(2,1)}, u32[]{:S(2)}) copy-start(bf16[32,768]{1,0:T(8,128)(2,1)} %param.21) | copy-start | bytes 147460
  228.4 78.2 %copy-start.3 = (f32[3072]{0:T(1024)S(1)}, f32[3072]{0:T(1024)}, u32[]{:S(2)}) copy-start(f32[3072]{0:T(1024)} %param.23) | copy-start | bytes 36868
  236.6 97.4 %all-gather.12.cloned.1.call-start = ((), (), s32[]{:S(2)}) async-start(), calls=%async_computation.5 | async-start | bytes 1966080 | tf_op jit(solution)/shard_map/all_gather | solution.py:189
  237.2 142.8 %all-gather.10.cloned.1.call-start = ((), (), s32[]{:S(2)}) async-start(), calls=%async_computation.4 | async-start | bytes 1622016 | tf_op jit(solution)/shard_map/all_gather | solution.py:188
  307.3 100.5 %all-gather.14.cloned.1.call-start = ((), (), s32[]{:S(2)}) async-start(), calls=%async_computation.6 | async-start | bytes 1966080 | tf_op jit(solution)/shard_map/all_gather | solution.py:190
  307.9 128.4 %all-gather.16.cloned.1.call-start = ((), (), s32[]{:S(2)}) async-start(), calls=%async_computation.7 | async-start | bytes 1966080 | tf_op jit(solution)/shard_map/all_gather | solution.py:191
  308.6 213.8 %reduce-scatter.2.cloned.1.call-start = ((), (), s32[]{:S(2)}) async-start(), calls=%async_computation.8 | async-start | bytes 3244032 | tf_op jit(solution)/shard_map/reduce_scatter | solution.py:195
  382.5 59.6 %copy-start.5 = (u32[128]{0:T(128)S(1)}, u32[128]{0:T(128)}, u32[]{:S(2)}) copy-start(u32[128]{0:T(128)} %constant.186) | copy-start | bytes 1540
  382.5 139.9 %copy-start.1 = (f32[3072]{0:T(1024)S(1)}, f32[3072]{0:T(1024)}, u32[]{:S(2)}) copy-start(f32[3072]{0:T(1024)} %param.28) | copy-start | bytes 36868
  382.5 139.9 %copy-start.2 = (f32[3072]{0:T(1024)S(1)}, f32[3072]{0:T(1024)}, u32[]{:S(2)}) copy-start(f32[3072]{0:T(1024)} %param.27) | copy-start | bytes 36868
  524.1 16.0 %all-to-all-start = ((bf16[8,4,768]{2,0,1:T(8,128)(2,1)}), bf16[8,4,768]{2,0,1:T(8,128)(2,1)S(1)}, u32[]{:S(2)}, u32[]{:S(2)}) async-start(bf16[8,4,768]{2,0,1:T(8,128)(2,1)} %bitcast.26), calls=%async_computation.1 | async-start | bytes 98304 | tf_op jit(solution)/shard_map/all_to_all | solution.py:207
Sparse Core Ops, SparseCore 0:
  16.9 45.5 all-gather.7
  130.9 76.9 all-gather.17
  236.7 68.5 all-reduce.2
  306.9 27.0 all-gather.11
  337.0 43.0 all-gather.9
  381.6 26.1 all-gather.13
  409.5 26.6 all-gather.15
  442.2 80.1 reduce-scatter.1
where the time goes:
time: 552 us; the launch traced here: 548 us
  waiting for transfers between devices  261 us (47%)
  local copies, waits for them, and re-layouts  178 us (32%)
  matrix products  38.7 us (7%)
  blocking collectives  24.9 us (5%)
  between operations  22.4 us (4%)
  other arithmetic  17.9 us (3%)
    reduce_scatter x1, waiting for transfers between devices, per_device(): lax.psum_scatter(jnp.dot(hidden_all, down_w, preferred_element_type=jnp.f...  79.1 us
    slice x2, local copies, waits for them, and re-layouts, per_device(): tail_cache[:, :, 1].reshape(conts_here, tail_cap, heads_here, HD)  54.9 us
    psum x1, waiting for transfers between devices, per_device(): lax.psum(jnp.dot(attn, w_out, preferred_element_type=jnp.float32), 'mlp')  54.6 us
    slice x2, local copies, waits for them, and re-layouts, per_device(): cache_values = prompt_cache[0, :, 1].reshape(span, heads_here, HD)  51.7 us
    all_gather x1, waiting for transfers between devices, per_device(): piece = lax.all_gather(normed_share, 'req', axis=0, tiled=True)  46 us
    slice x1, local copies, waits for them, and re-layouts, per_device(): tail_cache[:, :, 0].reshape(conts_here, tail_cap, heads_here, HD)  29.2 us
    all_gather x1, waiting for transfers between devices, per_device(): down_w = lax.all_gather(w_down, 'mlp', axis=0, tiled=True)  28.5 us
    slice x1, local copies, waits for them, and re-layouts, per_device(): cache_keys = prompt_cache[0, :, 0].reshape(span, heads_here, HD)  27.2 us
  transfers between devices with their start and end apart: 9, of which 6 were waited for; matrix products, arithmetic and copies ran while one was open for 33% of the time, Pallas kernels for 0%

commit v1 on v0

--- a/solution.py
+++ b/solution.py
@@ -7,6 +7,11 @@
 HD = 96
 norm_eps = 1e-05
 masked_value = -1e30
+
+
+def add_all(shard, axis):
+    parts = lax.all_gather(shard, axis)
+    return jnp.sum(parts, axis=0)
 
 
 def rotary(values, position):
@@ -178,7 +183,7 @@
     )
     attn = (row_numer / row_total[:, :, None]).astype(jnp.bfloat16).reshape(rows_here, width_here)
     residual_full = lax.all_gather(residual, "mlp", axis=1, tiled=True)
-    projected = lax.psum(jnp.dot(attn, w_out, preferred_element_type=jnp.float32), "mlp")
+    projected = add_all(jnp.dot(attn, w_out, preferred_element_type=jnp.float32), "mlp")
     state = residual_full.astype(jnp.float32) + projected
     mean_square = jnp.mean(state * state, axis=1, keepdims=True)
     normed = (state * lax.rsqrt(mean_square + norm_eps) * mlp_gain).astype(jnp.bfloat16)

time: 552 us -> 535 us (0.969)
  waiting for transfers between devices: 261 us -> 243 us
    psum x1 -> x0, waiting for transfers between devices: 54.6 us -> none  [per_device(): lax.psum(jnp.dot(attn, w_out, preferred_element_type=jnp.float32), 'mlp')]
    all_gather x0 -> x1, waiting for transfers between devices: none -> 38.9 us  [add_all(): parts = lax.all_gather(shard, axis)]
  transfers between devices with their start and end apart: 9 -> 9, of which waited for: 6 -> 6; matrix products, arithmetic and copies ran while one was open for 33% -> 34% of each run, Pallas kernels for 0% -> 0%
where the time goes in v1:
time: 535 us; the launch traced here: 531 us
  waiting for transfers between devices  243 us (45%)
  local copies, waits for them, and re-layouts  178 us (33%)
  matrix products  38.7 us (7%)
  blocking collectives  24.9 us (5%)
  between operations  22.4 us (4%)
  other arithmetic  18.5 us (3%)
    reduce_scatter x1, waiting for transfers between devices, per_device(): lax.psum_scatter(jnp.dot(hidden_all, down_w, preferred_element_type=jnp.f...  79.1 us
    slice x2, local copies, waits for them, and re-layouts, per_device(): tail_cache[:, :, 1].reshape(conts_here, tail_cap, heads_here, HD)  54.9 us
    slice x2, local copies, waits for them, and re-layouts, per_device(): cache_values = prompt_cache[0, :, 1].reshape(span, heads_here, HD)  51.7 us
    all_gather x1, waiting for transfers between devices, per_device(): piece = lax.all_gather(normed_share, 'req', axis=0, tiled=True)  45.7 us
    all_gather x1, waiting for transfers between devices, add_all(): parts = lax.all_gather(shard, axis)  38.9 us
    slice x1, local copies, waits for them, and re-layouts, per_device(): tail_cache[:, :, 0].reshape(conts_here, tail_cap, heads_here, HD)  29.2 us
    all_gather x1, waiting for transfers between devices, per_device(): down_w = lax.all_gather(w_down, 'mlp', axis=0, tiled=True)  28.4 us
    slice x1, local copies, waits for them, and re-layouts, per_device(): cache_keys = prompt_cache[0, :, 0].reshape(span, heads_here, HD)  27.2 us
  transfers between devices with their start and end apart: 9, of which 6 were waited for; matrix products, arithmetic and copies ran while one was open for 34% of the time, Pallas kernels for 0%

profile of v1, /device:TPU:0, one launch (start us, length us, event | category | flops | bytes accessed | tf_op | source)
XLA Modules:
  0.0 530.9 jit_solution(18153645477585577493)
XLA Ops:
  17.5 24.7 %fusion.44 = (bf16[1,4096,1,768]{3,2,1,0:T(2,128)(2,1)}, bf16[1,4096,1,768]{3,2,1,0:T(2,128)(2,1)}) fusion(bf16[1,4096,2,768]{3,2,1,0:T(2,128)(2,1)} %param.19), kind=kLoop, calls=%fused_computation.90 | loop fusion | bytes 25165824 | tf_op jit(solution)/shard_map/slice | solution.py:81
  42.2 27.2 %copy.87 = bf16[1,4096,1,768]{1,3,2,0:T(8,128)(2,1)} copy(bf16[1,4096,1,768]{3,2,1,0:T(2,128)(2,1)} %get-tuple-element.154) | data formatting | bytes 12582912 | tf_op jit(solution)/shard_map/slice | solution.py:80
  69.4 27.0 %copy.86 = bf16[1,4096,1,768]{1,3,2,0:T(8,128)(2,1)} copy(bf16[1,4096,1,768]{3,2,1,0:T(2,128)(2,1)} %get-tuple-element.153) | data formatting | bytes 12582912 | tf_op jit(solution)/shard_map/slice | solution.py:81
  97.5 4.2 broadcast_in_dim.60
  101.8 9.7 %while.22 = (s32[]{:T(128)}, f32[8,64,4096]{2,1,0:T(8,128)}, s32[]{:T(128)}, s32[]{:T(128)}, bf16[4096,8,96]{0,2,1:T(8,128)(2,1)}, /*index=5*/bf16[64,8,96]{2,0,...) while((s32[]{:T(128)}, f32[8,64,4096]{2,1,0:T(8,128)}, s32[]{:T(128)}, s32[]{:T(128)}, ...), condition=%wide.region_1.2_spmd, body=%wide.region_0.1_spmd.sunk | while | flops 50856964 | bytes 1935515 | solution.py:94
  111.4 3.8 reduce_max.27
  115.3 14.2 %while.23 = (s32[]{:T(128)}, f32[64,8,96]{2,0,1:T(8,128)S(1)}, f32[8,64]{1,0:T(8,128)S(1)}, s32[]{:T(128)}, bf16[4096,8,96]{0,2,1:T(8,128)(2,1)}, /*index=5*/f32...) while((s32[]{:T(128)}, f32[64,8,96]{2,0,1:T(8,128)S(1)}, ...), condition=%wide.region_5.6_spmd, body=%wide.region_3.5_spmd.sunk | while | flops 51429380 | bytes 3290271 | solution.py:114
  134.1 25.7 %fusion.43 = (bf16[16,256,1,768]{3,2,1,0:T(2,128)(2,1)}, bf16[16,256,1,768]{3,2,1,0:T(2,128)(2,1)}) fusion(bf16[16,256,2,768]{3,2,1,0:T(2,128)(2,1)} %param.20), kind=kLoop, calls=%fused_computation.89 | loop fusion | bytes 25165824 | tf_op jit(solution)/shard_map/slice | solution.py:141
  159.9 29.2 %copy.94 = bf16[16,256,1,768]{1,3,0,2:T(8,128)(2,1)} copy(bf16[16,256,1,768]{3,2,1,0:T(2,128)(2,1)} %get-tuple-element.152) | data formatting | bytes 12582912 | tf_op jit(solution)/shard_map/slice | solution.py:140
  190.1 3.8 fusion.48
  194.3 29.2 %copy.99 = bf16[16,256,1,768]{1,3,0,2:T(8,128)(2,1)} copy(bf16[16,256,1,768]{3,2,1,0:T(2,128)(2,1)} %get-tuple-element.151) | data formatting | bytes 12582912 | tf_op jit(solution)/shard_map/slice | solution.py:141
  223.8 4.6 fusion.15
  232.6 4.0 fusion.34
  237.3 13.5 %all_gather.30 = bf16[32,3072]{1,0:T(8,128)(2,1)S(1)} all-gather(bf16[32,768]{1,0:T(8,128)(2,1)S(1)} %copy-done), channel_id=1, replica_groups=mesh['req'=32,'mlp'=4] {'mlp'}, dimensions={1}, use_global_device_ids=true | all-gather | bytes 245760 | tf_op jit(solution)/shard_map/all_gather | solution.py:185
  250.7 38.9 %all-gather.22.cloned.1.call-done = f32[128,3072]{1,0:T(8,128)} async-done(((f32[32,3072]{1,0:T(8,128)}), f32[128,3072]{1,0:T(8,128)}) %all-gather.22.cloned.1.call-update) | async-done | bytes 1572880 | tf_op jit(solution)/shard_map/all_gather | solution.py:13
  293.5 24.3 %all-gather.14.cloned.1.call-done = bf16[3072,256]{0,1:T(8,128)(2,1)} async-done(((bf16[3072,64]{0,1:T(8,128)(2,1)}), bf16[3072,256]{0,1:T(8,128)(2,1)}) %all-gather.14.cloned.1.call-update) | async-done | bytes 1572880 | tf_op jit(solution)/shard_map/all_gather | solution.py:194
  317.8 45.7 %all-gather.12.cloned.1.call-done = bf16[256,3072]{1,0:T(8,128)(2,1)} async-done(((bf16[8,3072]{1,0:T(8,128)(2,1)}), bf16[256,3072]{1,0:T(8,128)(2,1)}) %all-gather.12.cloned.1.call-update) | async-done | bytes 1572880 | tf_op jit(solution)/shard_map/all_gather | solution.py:193
  363.5 2.5 fusion.49
  366.1 25.1 %all-gather.16.cloned.1.call-done = bf16[3072,256]{0,1:T(8,128)(2,1)} async-done(((bf16[3072,64]{0,1:T(8,128)(2,1)}), bf16[3072,256]{0,1:T(8,128)(2,1)}) %all-gather.16.cloned.1.call-update) | async-done | bytes 1572880 | tf_op jit(solution)/shard_map/all_gather | solution.py:195
  391.2 28.4 %all-gather.18.cloned.1.call-done = bf16[256,3072]{1,0:T(8,128)(2,1)} async-done(((bf16[64,3072]{1,0:T(8,128)(2,1)}), bf16[256,3072]{1,0:T(8,128)(2,1)}) %all-gather.18.cloned.1.call-update) | async-done | bytes 1572880 | tf_op jit(solution)/shard_map/all_gather | solution.py:196
  419.6 5.8 %fusion.14 = f32[256,3072]{1,0:T(8,128)} fusion(bf16[256,3072]{1,0:T(8,128)(2,1)} %all-gather.18.cloned.1.call-done, bf16[256,3072]{1,0:T(8,128)(2,1)} %all-gather.12.cloned.1.call-done, bf16[3072,256]{0,1:T(8,128)(2,1)} %all-gather.16.cloned.1.call-done, f32[256,256]{1,0:T(8,128)S(1)} %fusion.49), kind=kOutput, calls=%fused_computation.19 | convolution fusion | flops 805699584 | bytes 8126464 | tf_op jit(solution)/shard_map/dot_general | solution.py:201
  426.7 79.1 %reduce-scatter.2.cloned.1.call-done = f32[8,3072]{1,0:T(8,128)} async-done(((f32[256,3072]{1,0:T(8,128)}), f32[8,3072]{1,0:T(8,128)}) %reduce-scatter.2.cloned.1.call-update) | async-done | bytes 98320 | tf_op jit(solution)/shard_map/reduce_scatter | solution.py:200
  507.4 4.4 all-to-all-start
  512.0 11.4 %all-reduce = f32[32]{0:T(128)} all-reduce(f32[32]{0:T(128)S(1)} %multiply_dynamic-update-slice_fusion), channel_id=1, replica_groups=mesh['req'=32,'mlp'=4] {'mlp'}, use_global_device_ids=true, to_apply=%add | all-reduce | flops 32 | bytes 256
  (115 shorter events, 45.7 us)
Async XLA Ops:
  7.2 89.3 %all-gather.10.cloned.1.call-start = ((), (), s32[]{:S(2)}) async-start(), calls=%async_computation.2 | async-start | bytes 1622016 | tf_op jit(solution)/shard_map/all_gather | solution.py:63
  16.8 213.9 %all-gather.20.cloned.1.call-start = ((), (), s32[]{:S(2)}) async-start(), calls=%async_computation.8 | async-start | bytes 7569408 | tf_op jit(solution)/shard_map/all_gather | solution.py:123
  115.3 15.5 %copy-start.4 = (s32[32]{0:T(128)S(1)}, s32[32]{0:T(128)}, u32[]{:S(2)}) copy-start(s32[32]{0:T(128)} %param.29) | copy-start | bytes 388
  130.8 158.9 %all-gather.22.cloned.1.call-start = ((), (), s32[]{:S(2)}) async-start(), calls=%async_computation.9 | async-start | bytes 1966080 | tf_op jit(solution)/shard_map/all_gather | solution.py:13
  228.4 8.9 %copy-start = (bf16[32,768]{1,0:T(8,128)(2,1)S(1)}, bf16[32,768]{1,0:T(8,128)(2,1)}, u32[]{:S(2)}) copy-start(bf16[32,768]{1,0:T(8,128)(2,1)} %param.21) | copy-start | bytes 147460
  228.6 62.8 %copy-start.3 = (f32[3072]{0:T(1024)S(1)}, f32[3072]{0:T(1024)}, u32[]{:S(2)}) copy-start(f32[3072]{0:T(1024)} %param.23) | copy-start | bytes 36868
  236.6 81.2 %all-gather.14.cloned.1.call-start = ((), (), s32[]{:S(2)}) async-start(), calls=%async_computation.4 | async-start | bytes 1966080 | tf_op jit(solution)/shard_map/all_gather | solution.py:194
  237.2 126.3 %all-gather.12.cloned.1.call-start = ((), (), s32[]{:S(2)}) async-start(), calls=%async_computation.3 | async-start | bytes 1622016 | tf_op jit(solution)/shard_map/all_gather | solution.py:193
  292.1 99.1 %all-gather.16.cloned.1.call-start = ((), (), s32[]{:S(2)}) async-start(), calls=%async_computation.5 | async-start | bytes 1966080 | tf_op jit(solution)/shard_map/all_gather | solution.py:195
  292.7 126.9 %all-gather.18.cloned.1.call-start = ((), (), s32[]{:S(2)}) async-start(), calls=%async_computation.6 | async-start | bytes 1966080 | tf_op jit(solution)/shard_map/all_gather | solution.py:196
  293.5 212.3 %reduce-scatter.2.cloned.1.call-start = ((), (), s32[]{:S(2)}) async-start(), calls=%async_computation.7 | async-start | bytes 3244032 | tf_op jit(solution)/shard_map/reduce_scatter | solution.py:200
  366.0 59.4 %copy-start.5 = (u32[128]{0:T(128)S(1)}, u32[128]{0:T(128)}, u32[]{:S(2)}) copy-start(u32[128]{0:T(128)} %constant.186) | copy-start | bytes 1540
  366.1 139.7 %copy-start.1 = (f32[3072]{0:T(1024)S(1)}, f32[3072]{0:T(1024)}, u32[]{:S(2)}) copy-start(f32[3072]{0:T(1024)} %param.28) | copy-start | bytes 36868
  366.1 139.7 %copy-start.2 = (f32[3072]{0:T(1024)S(1)}, f32[3072]{0:T(1024)}, u32[]{:S(2)}) copy-start(f32[3072]{0:T(1024)} %param.27) | copy-start | bytes 36868
  507.4 16.0 %all-to-all-start = ((bf16[8,4,768]{2,0,1:T(8,128)(2,1)}), bf16[8,4,768]{2,0,1:T(8,128)(2,1)S(1)}, u32[]{:S(2)}, u32[]{:S(2)}) async-start(bf16[8,4,768]{2,0,1:T(8,128)(2,1)} %bitcast.27), calls=%async_computation.1 | async-start | bytes 98304 | tf_op jit(solution)/shard_map/all_to_all | solution.py:212
Sparse Core Ops, SparseCore 0:
  16.9 45.5 all-gather.9
  130.9 76.9 all-gather.19
  236.8 52.8 all-gather.21
  291.1 26.6 all-gather.13
  320.5 43.0 all-gather.11
  365.1 26.1 all-gather.15
  392.9 26.6 all-gather.17
  425.6 80.1 reduce-scatter.1
